TPU v7x, 32 devices: a whole 2x2x4 slice. The times are simulated.
32 devices in a mesh: ctx: 2 (over y), branch: 4 (over z), head: 4 (over x, core).
Axes of the slice: x: 2, y: 2, z: 4, core: 2. Of those that a mesh axis runs over, the one named last changes fastest.
Arguments:
- queries: bfloat16 [8, 128, 4096], P(('ctx', 'branch'), None, 'head'), may hold values from -320 to 320
- branch_keys: bfloat16 [8, 128, 512], P(('ctx', 'branch'), None, 'head'), may hold values from -12 to 12
- branch_value_rows: bfloat16 [8, 128, 512], P(('ctx', 'branch'), None, 'head'), may hold values from -6 to 6
- trunk_key_rows: bfloat16 [192, 512], P('ctx', 'head'), may hold values from -6 to 6
- trunk_value_rows: bfloat16 [192, 512], P('ctx', 'head'), may hold values from -6 to 6
- attn_out: bfloat16 [8, 128, 4096], P(('ctx', 'branch'), None, 'head'), may hold values from -2 to 2
- out_grad: bfloat16 [8, 128, 4096], P(('ctx', 'branch'), None, 'head'), may hold values from -6 to 6
- block_mask: int32 [8, 1, 3], P(('ctx', 'branch')), may hold values from 0 to 1, as said below
Outputs:
- query_grad: bfloat16 [8, 128, 4096], P(('ctx', 'branch'), None, 'head')
- branch_kv_grad: bfloat16 [8, 128, 1024], P(('ctx', 'branch'), None, 'head')
- trunk_kv_grad: bfloat16 [192, 1024], P(('ctx', 'branch'), 'head')
Inputs may be any that keep to these rules, and one draw needn't show every extreme that they name: `block_mask`: each entry is 0 or 1; columns 0 to 1 are the trunk's blocks, the rest the branch's own blocks, of which those on or above the query block's diagonal are not read. Every query block of every branch sees at least one trunk block. The share of ones differs from branch to branch.
All inputs are finite; a program needn't handle non-finite values.
Results may differ from a plain program's by a relative error of at most 0.017.
Values may be sent and summed in bfloat16 or wider, within the bound.
No kernel may reach another device: no remote copies, remote signals or barrier semaphores. Data moves between devices by JAX's collectives and lax.ppermute only.
A program may use at most 64 MiB of HBM per device.

v0:
```python
import math
import jax
import jax.numpy as jnp
from jax import lax
from jax.sharding import PartitionSpec as P

HEAD_WIDTH = 128
BLK = 128
masked_fill = -1e30


def head_scores(query_row_block, key_row_block, score_scale):
    return (
        jnp.einsum(
            "igd,kd->gik", query_row_block, key_row_block, preferred_element_type=jnp.float32
        )
        * score_scale
    )


def block_gradients(
    query_row_block,
    gradient_rows,
    key_row_block,
    value_rows,
    allowed,
    log_total,
    out_dot,
    score_scale,
):
    scores = head_scores(query_row_block, key_row_block, score_scale)
    weights = jnp.exp(jnp.where(allowed[None], scores, masked_fill) - log_total)
    weights_low = weights.astype(jnp.bfloat16)
    grad_weights = jnp.einsum(
        "igd,kd->gik", gradient_rows, value_rows, preferred_element_type=jnp.float32
    )
    grad_scores = (weights * (grad_weights - out_dot)).astype(jnp.bfloat16)
    query_portion = jnp.einsum(
        "gik,kd->igd", grad_scores, key_row_block, preferred_element_type=jnp.float32
    )
    key_gradient = (
        jnp.einsum("gik,igd->kd", grad_scores, query_row_block, preferred_element_type=jnp.float32)
        * score_scale
    )
    value_gradient = jnp.einsum(
        "gik,igd->kd", weights_low, gradient_rows, preferred_element_type=jnp.float32
    )
    return (query_portion, jnp.concatenate([key_gradient, value_gradient], axis=1))


def trunk_allowed(trunk_mask, offset, key_count, branch_len):
    tokens = offset + jnp.arange(key_count, dtype=jnp.int32)
    blocks = jnp.arange(trunk_mask.shape[1], dtype=jnp.int32)
    onehot = (tokens[None, :] // BLK == blocks[:, None]).astype(jnp.float32)
    visible = jnp.dot(trunk_mask, onehot, preferred_element_type=jnp.float32) > 0.5
    spread = jnp.broadcast_to(visible[:, None, :], (visible.shape[0], BLK, key_count))
    return spread.reshape(branch_len, key_count)


def branch_allowed(branch_mask, branch_len):
    block_count = branch_mask.shape[0]
    spread = jnp.broadcast_to(
        branch_mask[:, None, :, None] > 0, (block_count, BLK, block_count, BLK)
    ).reshape(branch_len, branch_len)
    position = jnp.arange(branch_len, dtype=jnp.int32)
    query_block = position[:, None] // BLK
    key_block = position[None, :] // BLK
    earlier = (key_block < query_block) & spread
    causal = (key_block == query_block) & (position[None, :] <= position[:, None])
    return earlier | causal


def shards(
    queries,
    branch_keys,
    branch_value_rows,
    trunk_key_rows,
    trunk_value_rows,
    attn_out,
    out_grad,
    block_mask,
):
    branch_len = queries.shape[1]
    group_width = queries.shape[2] // HEAD_WIDTH
    score_scale = 1.0 / math.sqrt(HEAD_WIDTH)
    query_row_block = queries[0].reshape(branch_len, group_width, HEAD_WIDTH)
    gradient_rows = out_grad[0].reshape(branch_len, group_width, HEAD_WIDTH)
    output_rows = attn_out[0].reshape(branch_len, group_width, HEAD_WIDTH)
    branch_own_keys = branch_keys[0]
    branch_own_values = branch_value_rows[0]
    mask_rows = block_mask[0]
    query_blocks = branch_len // BLK
    trunk_blocks = mask_rows.shape[1] - query_blocks
    trunk_mask = mask_rows[:, :trunk_blocks].astype(jnp.float32)
    own_allowed = branch_allowed(mask_rows[:, trunk_blocks:], branch_len)
    own_scores = jnp.where(
        own_allowed[None], head_scores(query_row_block, branch_own_keys, score_scale), masked_fill
    )
    row_max = jnp.max(own_scores, axis=2, keepdims=True)
    row_total = jnp.sum(jnp.exp(own_scores - row_max), axis=2, keepdims=True)
    trunk_rows, trunk_vals = (
        lax.all_gather(trunk_key_rows, "ctx", axis=0, tiled=True),
        lax.all_gather(trunk_value_rows, "ctx", axis=0, tiled=True),
    )
    trunk_len = trunk_rows.shape[0]
    block_len = math.gcd(512, trunk_len)
    block_total = trunk_len // block_len
    key_blocks = trunk_rows.reshape(block_total, block_len, HEAD_WIDTH)
    value_blocks = trunk_vals.reshape(block_total, block_len, HEAD_WIDTH)
    offsets = jnp.arange(block_total, dtype=jnp.int32) * block_len

    def stats_step(running, inputs):
        run_max, run_total = running
        key_block, offset = inputs
        allowed = trunk_allowed(trunk_mask, offset, block_len, branch_len)
        scores = jnp.where(
            allowed[None], head_scores(query_row_block, key_block, score_scale), masked_fill
        )
        new_max = jnp.maximum(run_max, jnp.max(scores, axis=2, keepdims=True))
        new_total = run_total * jnp.exp(run_max - new_max) + jnp.sum(
            jnp.exp(scores - new_max), axis=2, keepdims=True
        )
        return ((new_max, new_total), None)

    (row_max, row_total), ignored = lax.scan(
        stats_step, (row_max, row_total), (key_blocks, offsets)
    )
    log_total = row_max + jnp.log(row_total)
    out_dot = jnp.sum(
        gradient_rows.astype(jnp.float32) * output_rows.astype(jnp.float32), axis=2
    ).T[:, :, None]
    own_query, own_grad = block_gradients(
        query_row_block,
        gradient_rows,
        branch_own_keys,
        branch_own_values,
        own_allowed,
        log_total,
        out_dot,
        score_scale,
    )

    def grad_step(query_sum, inputs):
        key_block, value_block, offset = inputs
        allowed = trunk_allowed(trunk_mask, offset, block_len, branch_len)
        query_portion, key_value_pair = block_gradients(
            query_row_block,
            gradient_rows,
            key_block,
            value_block,
            allowed,
            log_total,
            out_dot,
            score_scale,
        )
        return (query_sum + query_portion, key_value_pair)

    query_sum, trunk_grad = lax.scan(grad_step, own_query, (key_blocks, value_blocks, offsets))
    query_out = (
        (query_sum * score_scale)
        .astype(jnp.bfloat16)
        .reshape(1, branch_len, group_width * HEAD_WIDTH)
    )
    branch_out = own_grad.astype(jnp.bfloat16)[None]
    trunk_term = lax.optimization_barrier(
        trunk_grad.reshape(trunk_len, 2 * HEAD_WIDTH).astype(jnp.bfloat16)
    ).astype(jnp.float32)
    reduced = lax.psum_scatter(
        trunk_term.astype(jnp.bfloat16), "ctx", scatter_dimension=0, tiled=True
    )
    trunk_out = lax.psum_scatter(reduced, "branch", scatter_dimension=0, tiled=True).astype(
        jnp.float32
    )
    return (query_out, branch_out, trunk_out.astype(jnp.bfloat16))


def solution(mesh):
    return jax.shard_map(
        shards,
        mesh=mesh,
        in_specs=(
            P(("ctx", "branch"), None, "head"),
            P(("ctx", "branch"), None, "head"),
            P(("ctx", "branch"), None, "head"),
            P("ctx", "head"),
            P("ctx", "head"),
            P(("ctx", "branch"), None, "head"),
            P(("ctx", "branch"), None, "head"),
            P(("ctx", "branch"), None, None),
        ),
        out_specs=(
            P(("ctx", "branch"), None, "head"),
            P(("ctx", "branch"), None, "head"),
            P(("ctx", "branch"), "head"),
        ),
        check_vma=False,
    )
```

profile of v0, /device:TPU:0, one launch (start us, length us, event | category | flops | bytes accessed | tf_op | source)
XLA Modules:
  0.0 79.4 jit_solution(5890720401216771830)
XLA Ops:
  7.2 0.6 copy-done.5
  7.8 0.6 slice.6
  8.5 5.7 %all_gather.6 = bf16[192,128]{1,0:T(8,128)(2,1)S(1)} all-gather(bf16[96,128]{1,0:T(8,128)(2,1)} %param.15), channel_id=1, replica_groups=mesh['ctx'=2,'branch'=4,'head'=4] {'ctx'}, dimensions={0}, use_global_device_ids=true | all-gather | bytes 73728 | tf_op jit(solution)/shard_map/all_gather | solution.py:102
  14.2 4.5 %all_gather.7 = bf16[192,128]{1,0:T(8,128)(2,1)S(1)} all-gather(bf16[96,128]{1,0:T(8,128)(2,1)S(1)} %copy-done.4), channel_id=1, replica_groups=mesh['ctx'=2,'branch'=4,'head'=4] {'ctx'}, dimensions={0}, use_global_device_ids=true | all-gather | bytes 73728 | tf_op jit(solution)/shard_map/all_gather | solution.py:103
  18.7 1.1 %copy.19 = bf16[1,128,1024]{1,2,0:T(8,128)(2,1)S(1)} copy(bf16[1,128,1024]{2,1,0:T(8,128)(2,1)} %param.12) | data formatting | bytes 524288 | tf_op args[0]
  20.0 0.8 copy-done.1
  20.9 0.8 copy-done.2
  23.3 5.1 %while.28 = (s32[]{:T(128)}, f32[8,128,1]{1,0,2:T(8,128)S(1)}, f32[8,128,1]{1,0,2:T(8,128)S(1)}, s32[3]{0:T(128)S(1)}, bf16[1,2]{1,0:T(2,128)(2,1)S(1)}, /*index...) while((s32[]{:T(128)}, f32[8,128,1]{1,0,2:T(8,128)S(1)}, ...), condition=%wide.region_5.6_spmd, body=%wide.region_2.5_spmd.sunk | while | flops 17108416 | bytes 857269 | solution.py:125
  23.3 0.6 dynamic_slice.57
  23.9 0.7 and_select_fusion.5
  25.0 0.6 dynamic_slice.57
  25.6 0.7 and_select_fusion.5
  26.7 0.6 dynamic_slice.57
  27.3 0.7 and_select_fusion.5
  28.6 0.3 convolution_bitcast_fusion.6
  29.1 9.3 %while.29 = (s32[]{:T(128)}, f32[128,8,128]{0,2,1:T(8,128)S(1)}, bf16[3,64,256]{2,1,0:T(8,128)(2,1)}, bf16[3,64,128]{2,1,0:T(8,128)(2,1)S(1)}, s32[3]{0:T(128)S(...) while((s32[]{:T(128)}, f32[128,8,128]{0,2,1:T(8,128)S(1)}, ...), condition=%wide.region_8.9_spmd, body=%wide.region_7.8_spmd.sunk | while | flops 84559296 | bytes 3433697 | solution.py:158
  29.1 0.6 dynamic_slice.61
  29.7 0.7 and_select_fusion.6
  31.3 0.6 fusion.114
  31.9 0.3 fusion.112
  32.2 0.6 dynamic_slice.61
  32.8 0.7 and_select_fusion.6
  34.4 0.6 fusion.114
  35.0 0.3 fusion.112
  35.3 0.6 dynamic_slice.61
  35.9 0.7 and_select_fusion.6
  37.5 0.6 fusion.114
  38.1 0.3 fusion.112
  39.1 11.4 %reduce-scatter.3.cloned.1.call-done = bf16[96,256]{1,0:T(8,128)(2,1)} async-done(((bf16[192,256]{1,0:T(8,128)(2,1)}), bf16[96,256]{1,0:T(8,128)(2,1)}) %reduce-scatter.3.cloned.1.call-update) | async-done | bytes 49168 | tf_op jit(solution)/shard_map/reduce_scatter | solution.py:168
  50.5 0.7 copy.32
  51.2 0.8 %copy.38 = bf16[1,128,1024]{2,1,0:T(8,128)(2,1)} copy(bf16[1,128,1024]{1,2,0:T(8,128)(2,1)S(1)} %bitcast.209) | data formatting | bytes 524288 | tf_op jit(solution)/shard_map/reshape | solution.py:162
  52.1 20.5 %reduce-scatter.5.cloned.1.call-done = bf16[24,256]{1,0:T(8,128)(2,1)} async-done(((bf16[96,256]{1,0:T(8,128)(2,1)}), bf16[24,256]{1,0:T(8,128)(2,1)}) %reduce-scatter.5.cloned.1.call-update) | async-done | bytes 12304 | tf_op jit(solution)/shard_map/reduce_scatter | solution.py:171
  (65 shorter events, 6.3 us)
Async XLA Ops:
  7.2 15.7 %copy-start = (bf16[1,128,128]{2,1,0:T(8,128)(2,1)S(1)}, bf16[1,128,128]{2,1,0:T(8,128)(2,1)}, u32[]{:S(2)}) copy-start(bf16[1,128,128]{2,1,0:T(8,128)(2,1)} %param.13) | copy-start | bytes 98308
  7.2 0.7 copy-start.5
  7.2 43.2 %reduce-scatter.3.cloned.1.call-start = ((), (), s32[]{:S(2)}) async-start(), calls=%async_computation.2 | async-start | bytes 147456 | tf_op jit(solution)/shard_map/reduce_scatter | solution.py:168
  8.4 5.7 %copy-start.4 = (bf16[96,128]{1,0:T(8,128)(2,1)S(1)}, bf16[96,128]{1,0:T(8,128)(2,1)}, u32[]{:S(2)}) copy-start(bf16[96,128]{1,0:T(8,128)(2,1)} %param.16) | copy-start | bytes 73732
  19.8 1.0 %copy-start.1 = (bf16[1,128,1024]{2,1,0:T(8,128)(2,1)S(1)}, bf16[1,128,1024]{2,1,0:T(8,128)(2,1)}, u32[]{:S(2)}) copy-start(bf16[1,128,1024]{2,1,0:T(8,128)(2,1)} %param.17) | copy-start | bytes 786436
  20.8 0.9 %copy-start.2 = (bf16[1,128,1024]{2,1,0:T(8,128)(2,1)S(1)}, bf16[1,128,1024]{2,1,0:T(8,128)(2,1)}, u32[]{:S(2)}) copy-start(bf16[1,128,1024]{2,1,0:T(8,128)(2,1)} %param.18) | copy-start | bytes 786436
  23.2 5.2 %copy-start.3 = (bf16[1,128,128]{2,1,0:T(8,128)(2,1)S(1)}, bf16[1,128,128]{2,1,0:T(8,128)(2,1)}, u32[]{:S(2)}) copy-start(bf16[1,128,128]{2,1,0:T(8,128)(2,1)} %param.14) | copy-start | bytes 98308
  38.4 34.1 %reduce-scatter.5.cloned.1.call-start = ((), (), s32[]{:S(2)}) async-start(), calls=%async_computation.3 | async-start | bytes 61440 | tf_op jit(solution)/shard_map/reduce_scatter | solution.py:171
Sparse Core Ops, SparseCore 0:
  38.6 11.8 reduce-scatter.2
  53.2 19.2 reduce-scatter.4
where the time goes:
time: 79.8 us; the launch traced here: 79.4 us
  waiting for transfers between devices  31.9 us (40%)
  between operations  14.9 us (19%)
  blocking collectives  10.2 us (13%)
  local copies, waits for them, and re-layouts  9.88 us (12%)
  other arithmetic  6.35 us (8%)
  matrix products  5.74 us (7%)
    reduce_scatter x1, waiting for transfers between devices, shards(): lax.psum_scatter(reduced, 'branch', scatter_dimension=0, tiled=True)  20.5 us
    reduce_scatter x1, waiting for transfers between devices, shards(): lax.psum_scatter(trunk_term.astype(jnp.bfloat16), 'ctx', scatter_dimensio...  11.4 us
    all_gather x1, blocking collectives, shards(): lax.all_gather(trunk_key_rows, 'ctx', axis=0, tiled=True)  5.73 us
    all_gather x1, blocking collectives, shards(): lax.all_gather(trunk_value_rows, 'ctx', axis=0, tiled=True)  4.48 us
    unnamed x16, local copies, waits for them, and re-layouts  4.36 us
    select_n x6, other arithmetic, trunk_allowed(): onehot = (tokens[None, :] // BLK == blocks[:, None]).astype(jnp.float32)  3.92 us
    dynamic_slice x6, local copies, waits for them, and re-layouts, shards(): lax.scan(stats_step, (row_max, row_total), (key_blocks, offsets))  3.52 us
    dynamic_update_slice x3, other arithmetic, shards(): lax.scan(grad_step, own_query, (key_blocks, value_blocks, offsets))  1.88 us
  transfers between devices with their start and end apart: 2, of which 2 were waited for; matrix products, arithmetic and copies ran while one was open for 3% of the time, Pallas kernels for 0%

commit v1 on v0

--- a/solution.py
+++ b/solution.py
@@ -7,6 +7,18 @@
 HEAD_WIDTH = 128
 BLK = 128
 masked_fill = -1e30
+
+
+def gather_by_bits(array, axis, dim):
+    ways, here, step = (lax.axis_size(axis), lax.axis_index(axis), array.shape[dim])
+    line, have = (array, 1)
+    while have < ways:
+        line = jnp.concatenate(
+            [line, lax.ppermute(line, axis, [(d, (d - have) % ways) for d in range(ways)])],
+            axis=dim,
+        )
+        have = 2 * have
+    return jnp.roll(line, here * step, axis=dim)
 
 
 def head_scores(query_row_block, key_row_block, score_scale):
@@ -99,7 +111,7 @@
     row_max = jnp.max(own_scores, axis=2, keepdims=True)
     row_total = jnp.sum(jnp.exp(own_scores - row_max), axis=2, keepdims=True)
     trunk_rows, trunk_vals = (
-        lax.all_gather(trunk_key_rows, "ctx", axis=0, tiled=True),
+        gather_by_bits(trunk_key_rows, "ctx", 0),
         lax.all_gather(trunk_value_rows, "ctx", axis=0, tiled=True),
     )
     trunk_len = trunk_rows.shape[0]

time: 79.8 us -> 76.9 us (0.964)
  blocking collectives: 10.2 us -> 4.61 us
  starting transfers between devices: 0.08 us -> 3.14 us
  waiting for transfers between devices: 31.9 us -> 31 us
    all_gather x1 -> x0, blocking collectives: 5.73 us -> none  [shards(): lax.all_gather(trunk_key_rows, 'ctx', axis=0, tiled=True)]
    ppermute x0 -> x1, starting transfers between devices: none -> 3.06 us  [gather_by_bits(): lax.ppermute(line, axis, [(d, (d - have) % ways) for d in range(ways)])]
    reduce_scatter x1, waiting for transfers between devices: 11.4 us -> 10.5 us  [shards(): lax.psum_scatter(trunk_term.astype(jnp.bfloat16), 'ctx', scatter_dimensio...]
    unnamed x16 -> x18, local copies, waits for them, and re-layouts: 4.36 us -> 4.07 us
  transfers between devices with their start and end apart: 2 -> 3, of which waited for: 2 -> 2; matrix products, arithmetic and copies ran while one was open for 3% -> 6% of each run, Pallas kernels for 0% -> 0%
where the time goes in v1:
time: 76.9 us; the launch traced here: 76.4 us
  waiting for transfers between devices  31 us (40%)
  between operations  14.9 us (19%)
  local copies, waits for them, and re-layouts  9.82 us (13%)
  other arithmetic  6.83 us (9%)
  matrix products  5.74 us (7%)
  blocking collectives  4.61 us (6%)
  starting transfers between devices  3.14 us (4%)
    reduce_scatter x1, waiting for transfers between devices, shards(): lax.psum_scatter(reduced, 'branch', scatter_dimension=0, tiled=True)  20.5 us
    reduce_scatter x1, waiting for transfers between devices, shards(): lax.psum_scatter(trunk_term.astype(jnp.bfloat16), 'ctx', scatter_dimensio...  10.5 us
    all_gather x1, blocking collectives, shards(): lax.all_gather(trunk_value_rows, 'ctx', axis=0, tiled=True)  4.61 us
    unnamed x18, local copies, waits for them, and re-layouts  4.07 us
    select_n x6, other arithmetic, trunk_allowed(): onehot = (tokens[None, :] // BLK == blocks[:, None]).astype(jnp.float32)  4.05 us
    dynamic_slice x6, local copies, waits for them, and re-layouts, shards(): lax.scan(stats_step, (row_max, row_total), (key_blocks, offsets))  3.76 us
    ppermute x1, starting transfers between devices, gather_by_bits(): lax.ppermute(line, axis, [(d, (d - have) % ways) for d in range(ways)])  3.06 us
    dynamic_update_slice x3, other arithmetic, shards(): lax.scan(grad_step, own_query, (key_blocks, value_blocks, offsets))  1.88 us
  transfers between devices with their start and end apart: 3, of which 2 were waited for; matrix products, arithmetic and copies ran while one was open for 6% of the time, Pallas kernels for 0%

profile of v1, /device:TPU:0, one launch (start us, length us, event | category | flops | bytes accessed | tf_op | source)
XLA Modules:
  0.0 76.4 jit_solution(5417785233440600571)
XLA Ops:
  7.2 3.1 %collective-permute-start = (bf16[96,128]{1,0:T(8,128)(2,1)}, bf16[96,128]{1,0:T(8,128)(2,1)S(1)}, u32[]{:S(2)}, u32[]{:S(2)}) collective-permute-start(bf16[96,128]{1,0:T(8,128)(2,1)} %param.15), channel_id=1, source_target_pairs={{0,16},{16,0},{1,17},{17,1},{2,18},{18,2},{3,19},{19,3},{4,20},{20... | collective-permute-start | bytes 73736 | tf_op jit(solution)/shard_map/ppermute | solution.py:17
  10.3 0.6 slice.6
  10.9 1.2 %copy.19 = bf16[1,128,1024]{1,2,0:T(8,128)(2,1)S(1)} copy(bf16[1,128,1024]{2,1,0:T(8,128)(2,1)} %param.12) | data formatting | bytes 524288 | tf_op args[0]
  12.3 0.8 %copy-done.2 = bf16[1,128,1024]{2,1,0:T(8,128)(2,1)S(1)} copy-done((bf16[1,128,1024]{2,1,0:T(8,128)(2,1)S(1)}, bf16[1,128,1024]{2,1,0:T(8,128)(2,1)}, u32[]{:S(2)}) %copy-start.2) | copy-done | bytes 262168
  14.8 0.5 copy-done.4
  15.3 4.6 %all_gather.3 = bf16[192,128]{1,0:T(8,128)(2,1)S(1)} all-gather(bf16[96,128]{1,0:T(8,128)(2,1)S(1)} %copy-done.4), channel_id=1, replica_groups=mesh['ctx'=2,'branch'=4,'head'=4] {'ctx'}, dimensions={0}, use_global_device_ids=true | all-gather | bytes 73728 | tf_op jit(solution)/shard_map/all_gather | solution.py:115
  20.0 0.4 fusion.53
  20.3 5.5 %while.28 = (s32[]{:T(128)}, f32[8,128,1]{1,0,2:T(8,128)S(1)}, f32[8,128,1]{1,0,2:T(8,128)S(1)}, s32[3]{0:T(128)S(1)}, bf16[1,2]{1,0:T(2,128)(2,1)S(1)}, /*index...) while((s32[]{:T(128)}, f32[8,128,1]{1,0,2:T(8,128)S(1)}, ...), condition=%wide.region_5.6_spmd, body=%wide.region_2.5_spmd.sunk | while | flops 17108416 | bytes 857269 | solution.py:137
  20.3 0.7 dynamic_slice.82
  21.0 0.7 and_select_fusion.5
  22.2 0.7 dynamic_slice.82
  22.8 0.7 and_select_fusion.5
  24.0 0.7 dynamic_slice.82
  24.7 0.7 and_select_fusion.5
  26.1 0.5 copy-done.3
  27.5 9.3 %while.29 = (s32[]{:T(128)}, f32[128,8,128]{0,2,1:T(8,128)S(1)}, bf16[3,64,256]{2,1,0:T(8,128)(2,1)}, bf16[3,64,128]{2,1,0:T(8,128)(2,1)S(1)}, s32[3]{0:T(128)S(...) while((s32[]{:T(128)}, f32[128,8,128]{0,2,1:T(8,128)S(1)}, ...), condition=%wide.region_8.9_spmd, body=%wide.region_7.8_spmd.sunk | while | flops 84559296 | bytes 3433697 | solution.py:170
  27.5 0.6 dynamic_slice.86
  28.1 0.7 and_select_fusion.6
  29.7 0.6 fusion.117
  30.4 0.3 fusion.115
  30.6 0.6 dynamic_slice.86
  31.2 0.7 and_select_fusion.6
  32.8 0.6 fusion.117
  33.5 0.3 fusion.115
  33.7 0.6 dynamic_slice.86
  34.3 0.7 and_select_fusion.6
  35.9 0.6 fusion.117
  36.6 0.3 fusion.115
  37.0 10.5 %reduce-scatter.3.cloned.1.call-done = bf16[96,256]{1,0:T(8,128)(2,1)} async-done(((bf16[192,256]{1,0:T(8,128)(2,1)}), bf16[96,256]{1,0:T(8,128)(2,1)}) %reduce-scatter.3.cloned.1.call-update) | async-done | bytes 49168 | tf_op jit(solution)/shard_map/reduce_scatter | solution.py:180
  47.5 0.7 copy.32
  48.2 0.8 %copy.38 = bf16[1,128,1024]{2,1,0:T(8,128)(2,1)} copy(bf16[1,128,1024]{1,2,0:T(8,128)(2,1)S(1)} %bitcast.209) | data formatting | bytes 524288 | tf_op jit(solution)/shard_map/reshape | solution.py:174
  49.1 20.5 %reduce-scatter.5.cloned.1.call-done = bf16[24,256]{1,0:T(8,128)(2,1)} async-done(((bf16[96,256]{1,0:T(8,128)(2,1)}), bf16[24,256]{1,0:T(8,128)(2,1)}) %reduce-scatter.5.cloned.1.call-update) | async-done | bytes 12304 | tf_op jit(solution)/shard_map/reduce_scatter | solution.py:183
  (69 shorter events, 6.5 us)
Async XLA Ops:
  7.2 6.9 %copy-start = (bf16[1,128,128]{2,1,0:T(8,128)(2,1)S(1)}, bf16[1,128,128]{2,1,0:T(8,128)(2,1)}, u32[]{:S(2)}) copy-start(bf16[1,128,128]{2,1,0:T(8,128)(2,1)} %param.13) | copy-start | bytes 98308
  7.2 3.1 %copy-start.6 = (s32[1,1,3]{2,1,0:T(1,128)S(1)}, s32[1,1,3]{2,1,0:T(1,128)}, u32[]{:S(2)}) copy-start(s32[1,1,3]{2,1,0:T(1,128)} %param.19) | copy-start | bytes 40
  7.2 40.3 %reduce-scatter.3.cloned.1.call-start = ((), (), s32[]{:S(2)}) async-start(), calls=%async_computation.2 | async-start | bytes 147456 | tf_op jit(solution)/shard_map/reduce_scatter | solution.py:180
  7.2 12.7 %collective-permute-start = (bf16[96,128]{1,0:T(8,128)(2,1)}, bf16[96,128]{1,0:T(8,128)(2,1)S(1)}, u32[]{:S(2)}, u32[]{:S(2)}) collective-permute-start(bf16[96,128]{1,0:T(8,128)(2,1)} %param.15), channel_id=1, source_target_pairs={{0,16},{16,0},{1,17},{17,1},{2,18},{18,2},{3,19},{19,3},{4,20},{20... | collective-permute-start | bytes 73736 | tf_op jit(solution)/shard_map/ppermute | solution.py:17
  10.9 1.2 %copy-start.1 = (bf16[1,128,1024]{2,1,0:T(8,128)(2,1)S(1)}, bf16[1,128,1024]{2,1,0:T(8,128)(2,1)}, u32[]{:S(2)}) copy-start(bf16[1,128,1024]{2,1,0:T(8,128)(2,1)} %param.17) | copy-start | bytes 786436
  12.1 1.0 %copy-start.2 = (bf16[1,128,1024]{2,1,0:T(8,128)(2,1)S(1)}, bf16[1,128,1024]{2,1,0:T(8,128)(2,1)}, u32[]{:S(2)}) copy-start(bf16[1,128,1024]{2,1,0:T(8,128)(2,1)} %param.18) | copy-start | bytes 786436
  14.6 0.7 copy-start.4
  15.3 4.6 %copy-start.5 = (bf16[96,128]{1,0:T(8,128)(2,1)S(1)}, bf16[96,128]{1,0:T(8,128)(2,1)}, u32[]{:S(2)}) copy-start(bf16[96,128]{1,0:T(8,128)(2,1)} %param.15) | copy-start | bytes 73732
  25.8 0.8 copy-start.3
  36.9 32.7 %reduce-scatter.5.cloned.1.call-start = ((), (), s32[]{:S(2)}) async-start(), calls=%async_computation.3 | async-start | bytes 61440 | tf_op jit(solution)/shard_map/reduce_scatter | solution.py:183
Sparse Core Ops, SparseCore 0:
  37.0 10.4 reduce-scatter.2
  50.3 19.2 reduce-scatter.4
